TPU v7x, 256 devices: a whole 4x4x8 slice. The times are simulated.
256 devices in a mesh: net: 32 (over x, z), scen: 8 (over y, core).
Axes of the slice: x: 4, y: 4, z: 8, core: 2. Of those that a mesh axis runs over, the one named last changes fastest.
Arguments:
- arc_flows: float32 [256, 262144], P('scen', 'net'), may hold values from 0 to 1
- node_duals: float32 [256, 65536], P('scen', 'net'), may hold values from -6 to 6
- demand: float32 [256, 65536], P('scen', 'net'), may hold values from -6 to 6
- excess: float32 [256], P('scen'), may hold values from 0 to 0.5
- risk_duals: float32 [256], P('scen'), may hold values from 0.2 to 6
- threshold: float32 [1], replicated, may hold values from -2.5 to -1.5
- arc_costs: float32 [262144], P('net'), may hold values from 0.05 to 0.75
- local_blocks: bfloat16 [2048, 4, 128, 128], P('net'), may hold values from -0.125 to 0.125
- head_blocks: bfloat16 [2048, 128, 128], P('net'), may hold values from -0.125 to 0.125
- local_index: int32 [2048, 4], P('net'), may hold values from 0 to 15
- head_index: int32 [2048], P('net'), may hold values from 0 to 511, as said below
Outputs:
- flows_next: float32 [256, 262144], P('scen', 'net')
- duals_next: float32 [256, 65536], P('scen', 'net')
- excess_next: float32 [256], P('scen')
- risk_next: float32 [256], P('scen')
- threshold_next: float32 [1], replicated
Inputs may be any that keep to these rules, and one draw needn't show every extreme that they name: Among the arc blocks of one device, at most 4 have their head node block on any one device of net (head_index // 16 names the device), and in every device's arc blocks some device of net is named exactly 4 times.
All inputs are finite; a program needn't handle non-finite values.
Results may differ from a plain program's by a relative error of at most 0.0021.
Values may be sent and summed in bfloat16 or wider, within the bound.
A program may use at most 128 MiB of HBM per device.

v0:
```python
import jax
import jax.numpy as jnp
from jax import lax
from jax.sharding import PartitionSpec as P

ROUNDS = 3
primal_step = 0.5
dual_step = 0.5
risk_step = 1.0
tail_weight = 2.0


def per_device(
    arc_flows,
    node_duals,
    demand,
    excess,
    risk_duals,
    threshold,
    arc_costs,
    local_blocks,
    head_blocks,
    local_index,
    head_index,
):
    block_rows = local_blocks.shape[-1]
    scen_rows = arc_flows.shape[0]
    arc_blks = head_index.shape[0]
    node_blks = node_duals.shape[1] // block_rows
    touches = local_index.shape[1]
    net_size = lax.axis_size("net")
    scen_size = lax.axis_size("scen")
    slot_cap = max(2, (2 * arc_blks + net_size - 1) // net_size)
    slot_count = net_size * slot_cap
    arc_total = arc_flows.shape[1] * net_size
    scen_total = scen_rows * scen_size
    select_prec = lax.Precision.HIGH
    peer_dev = head_index // node_blks
    target = head_index % node_blks
    peer_hot = (peer_dev[:, None] == jnp.arange(net_size, dtype=jnp.int32)[None, :]).astype(
        jnp.int32
    )
    earlier = jnp.cumsum(peer_hot, axis=0) - peer_hot
    slot_rank = jnp.sum(earlier * peer_hot, axis=1)
    slot_ids = peer_dev * slot_cap + slot_rank
    slot_hot = slot_ids[:, None] == jnp.arange(slot_count, dtype=jnp.int32)[None, :]
    arc_ids = jnp.arange(arc_blks, dtype=jnp.int32)
    slot_arc = jnp.max(jnp.where(slot_hot, arc_ids[:, None], -1), axis=0)
    slot_filled = slot_arc >= 0
    slot_source = jnp.maximum(slot_arc, 0)
    wanted = jnp.max(jnp.where(slot_hot, target[:, None], -1), axis=0).reshape(net_size, slot_cap)
    asked = lax.all_to_all(wanted, "net", split_axis=0, concat_axis=0, tiled=True)
    asked_hot = asked.reshape(-1)[:, None] == jnp.arange(node_blks, dtype=jnp.int32)[None, :]
    local_hot = local_index[:, :, None] == jnp.arange(node_blks, dtype=jnp.int32)[None, None, :]
    asked_wide = asked_hot.astype(jnp.float32)
    local_wide = local_hot.astype(jnp.float32)
    local_half = local_hot.astype(jnp.bfloat16)
    flow_now = arc_flows
    dual_now = node_duals
    level = threshold
    excess_now = excess
    risk_now = risk_duals
    for iteration in range(ROUNDS):
        dual_panel = dual_now.astype(jnp.bfloat16)
        dual_grid = dual_panel.reshape(scen_rows, node_blks, block_rows)
        gathered = lax.all_gather(dual_panel, "net", axis=1, tiled=True)
        head_rows = jnp.take(gathered.reshape(scen_rows, -1, block_rows), head_index, axis=1)
        pull_summed = jnp.einsum(
            "sjn,jmn->sjm", head_rows, head_blocks, preferred_element_type=jnp.float32
        )
        for touched in range(touches):
            local_rows = jnp.einsum(
                "sbn,jb->sjn", dual_grid, local_half[:, touched], preferred_element_type=jnp.float32
            ).astype(jnp.bfloat16)
            pull_summed = pull_summed + jnp.einsum(
                "sjn,jmn->sjm",
                local_rows,
                local_blocks[:, touched],
                preferred_element_type=jnp.float32,
            )
        pulled = pull_summed.reshape(scen_rows, arc_blks * block_rows)
        risk_mine = risk_now
        mean_risk = lax.psum(jnp.sum(risk_now), "scen") / scen_total
        flows_new = jnp.maximum(
            flow_now - primal_step * (risk_mine[:, None] * arc_costs[None, :] - pulled), 0.0
        )
        level_new = level - primal_step * (1.0 - mean_risk)
        flows_bar = 2.0 * flows_new - flow_now
        level_bar = 2.0 * level_new - level
        partial_value = jnp.sum(arc_costs[None, :] * flows_bar, axis=1) / arc_total
        excess_new = jnp.maximum(excess_now - primal_step * (tail_weight - risk_now), 0.0)
        excess_bar = 2.0 * excess_new - excess_now
        losses = lax.psum(partial_value, "net")
        risk_now = jnp.maximum(risk_now + risk_step * (losses - excess_bar - level_bar), 0.0)
        excess_now = excess_new
        flow_grid = flows_bar.astype(jnp.bfloat16).reshape(scen_rows, arc_blks, block_rows)
        own_terms = jnp.einsum(
            "sjm,jmn->sjn", flow_grid, head_blocks, preferred_element_type=jnp.float32
        )
        term_pack = jnp.where(
            slot_filled[None, :, None], jnp.take(own_terms, slot_source, axis=1), 0.0
        )
        arrived = lax.all_to_all(
            term_pack.reshape(scen_rows, net_size, slot_cap, block_rows),
            "net",
            split_axis=1,
            concat_axis=1,
            tiled=True,
        )
        head_terms = arrived.reshape(scen_rows, slot_count, block_rows)
        summed = jnp.einsum("sqn,qb->sbn", head_terms, asked_wide, precision=select_prec)
        local_terms = jnp.einsum(
            "sjm,jkmn->sjkn", flow_grid, local_blocks, preferred_element_type=jnp.float32
        )
        summed = summed + jnp.einsum(
            "sjkn,jkb->sbn", local_terms, local_wide, precision=select_prec
        )
        dual_now = dual_now + dual_step * (
            demand - summed.reshape(scen_rows, node_blks * block_rows)
        )
        flow_now = flows_new
        level = level_new
    return (flow_now, dual_now, excess_now, risk_now, level)


def solution(mesh):
    placed = (
        P("scen", "net"),
        P("scen", "net"),
        P("scen", "net"),
        P("scen"),
        P("scen"),
        P(),
        P("net"),
        P("net", None, None, None),
        P("net", None, None),
        P("net", None),
        P("net"),
    )
    return jax.shard_map(
        per_device,
        mesh=mesh,
        in_specs=placed,
        out_specs=(P("scen", "net"), P("scen", "net"), P("scen"), P("scen"), P()),
        check_vma=False,
    )
```

profile of v0, /device:TPU:0, one launch (start us, length us, event | category | flops | bytes accessed | tf_op | source)
XLA Modules:
  0.0 597.3 jit_solution(4962526115088580452)
XLA Ops:
  10.9 9.6 %all-to-all-start = ((s32[32,1,4]{2,1,0:T(1,128)}), s32[32,1,4]{2,1,0:T(1,128)S(1)}, u32[]{:S(2)}, u32[]{:S(2)}) async-start(s32[32,1,4]{2,1,0:T(1,128)} %bitcast.20), calls=%async_computation | async-start | bytes 32768 | tf_op jit(solution)/shard_map/all_to_all | solution.py:52
  27.9 3.8 fusion.16
  31.7 3.9 fusion.22
  35.6 58.6 %all-gather.4.cloned.1.call-done = bf16[32,65536]{1,0:T(8,128)(2,1)} async-done(((bf16[32,2048]{1,0:T(8,128)(2,1)}), bf16[32,65536]{1,0:T(8,128)(2,1)}) %all-gather.4.cloned.1.call-update) | async-done | bytes 4194320 | tf_op jit(solution)/shard_map/all_gather | solution.py:66
  94.2 4.9 copy_bitcast_fusion.2
  116.7 5.4 all-to-all-start.1
  125.6 4.8 convolution_bitcast_fusion.2
  133.5 36.8 %all-to-all-done.1 = f32[32,32,4,128]{3,0,2,1:T(8,128)} async-done(((f32[32,32,4,128]{3,0,2,1:T(8,128)}), f32[32,32,4,128]{3,0,2,1:T(8,128)}, u32[]{:S(2)}, u32[]{:S(2)}) %all-to-all-start.1) | async-done | bytes 2097184 | tf_op jit(solution)/shard_map/all_to_all | solution.py:103
  175.8 13.0 %psum.43 = f32[]{:T(128)} all-reduce(f32[]{:T(128)} %reduce_sum.64), channel_id=1, replica_groups=mesh['net'=32,'scen'=8] {'scen'}, use_global_device_ids=true, to_apply=%region_3.5 | all-reduce | flops 1 | bytes 8 | tf_op jit(solution)/shard_map/psum | solution.py:83
  190.2 72.1 %psum.42 = f32[32]{0:T(128)S(1)} all-reduce(f32[32]{0:T(128)S(1)} %broadcast_multiply_fusion.2), channel_id=1, replica_groups=mesh['net'=32,'scen'=8] {'net'}, use_global_device_ids=true, to_apply=%region_1.3 | all-reduce | flops 32 | bytes 256 | tf_op jit(solution)/shard_map/psum | solution.py:93
  268.9 3.9 fusion.14
  276.5 4.9 copy_bitcast_fusion.1
  299.0 4.8 all-to-all-start.2
  305.5 4.8 convolution_bitcast_fusion.1
  314.1 26.1 %all-to-all-done.2 = f32[32,32,4,128]{3,0,2,1:T(8,128)} async-done(((f32[32,32,4,128]{3,0,2,1:T(8,128)}), f32[32,32,4,128]{3,0,2,1:T(8,128)}, u32[]{:S(2)}, u32[]{:S(2)}) %all-to-all-start.2) | async-done | bytes 2097184 | tf_op jit(solution)/shard_map/all_to_all | solution.py:103
  345.3 13.1 %psum.45 = f32[]{:T(128)} all-reduce(f32[]{:T(128)} %get-tuple-element.16), channel_id=1, replica_groups=mesh['net'=32,'scen'=8] {'scen'}, use_global_device_ids=true, to_apply=%region_11.14 | all-reduce | flops 1 | bytes 8 | tf_op jit(solution)/shard_map/psum | solution.py:83
  359.1 74.1 %psum.44 = f32[32]{0:T(128)S(1)} all-reduce(f32[32]{0:T(128)S(1)} %broadcast_multiply_fusion.1), channel_id=1, replica_groups=mesh['net'=32,'scen'=8] {'net'}, use_global_device_ids=true, to_apply=%region_9.12 | all-reduce | flops 32 | bytes 256 | tf_op jit(solution)/shard_map/psum | solution.py:93
  436.9 3.8 fusion.6
  440.7 3.9 fusion.12
  448.4 4.9 copy_bitcast_fusion
  471.7 4.8 all-to-all-start.3
  476.4 13.9 %psum.47 = f32[]{:T(128)} all-reduce(f32[]{:T(128)} %get-tuple-element.11), channel_id=1, replica_groups=mesh['net'=32,'scen'=8] {'scen'}, use_global_device_ids=true, to_apply=%region_15.18 | all-reduce | flops 1 | bytes 8 | tf_op jit(solution)/shard_map/psum | solution.py:83
  492.4 83.1 %psum.46 = f32[32]{0:T(128)S(1)} all-reduce(f32[32]{0:T(128)S(1)} %broadcast_multiply_fusion), channel_id=1, replica_groups=mesh['net'=32,'scen'=8] {'net'}, use_global_device_ids=true, to_apply=%region_13.16 | all-reduce | flops 32 | bytes 256 | tf_op jit(solution)/shard_map/psum | solution.py:93
  576.1 4.8 convolution_bitcast_fusion
  (151 shorter events, 114.9 us)
Async XLA Ops:
  7.2 95.6 %copy-start = (bf16[64,128,128]{2,1,0:T(8,128)(2,1)S(1)}, bf16[64,128,128]{2,1,0:T(8,128)(2,1)}, u32[]{:S(2)}) copy-start(bf16[64,128,128]{2,1,0:T(8,128)(2,1)} %param.23) | copy-start | bytes 6291460
  7.2 87.1 %all-gather.4.cloned.1.call-start = ((), (), s32[]{:S(2)}) async-start(), calls=%async_computation.4 | async-start | bytes 4325376 | tf_op jit(solution)/shard_map/all_gather | solution.py:66
  10.9 105.9 %all-to-all-start = ((s32[32,1,4]{2,1,0:T(1,128)}), s32[32,1,4]{2,1,0:T(1,128)S(1)}, u32[]{:S(2)}, u32[]{:S(2)}) async-start(s32[32,1,4]{2,1,0:T(1,128)} %bitcast.20), calls=%async_computation | async-start | bytes 32768 | tf_op jit(solution)/shard_map/all_to_all | solution.py:52
  102.7 2.4 copy-start.11
  102.7 2.5 copy-start.22
  105.2 3.0 copy-start.3
  105.2 3.0 copy-start.25
  105.2 3.0 copy-start.27
  108.8 15.3 %copy-start.1 = (f32[32,8192]{1,0:T(8,128)}, f32[32,8192]{1,0:T(8,128)S(1)}, u32[]{:S(2)}) copy-start(f32[32,8192]{1,0:T(8,128)S(1)} %get-tuple-element.21) | copy-start | bytes 3145732
  116.7 53.5 %all-to-all-start.1 = ((f32[32,32,4,128]{3,0,2,1:T(8,128)}), f32[32,32,4,128]{3,0,2,1:T(8,128)}, u32[]{:S(2)}, u32[]{:S(2)}) async-start(f32[32,32,4,128]{3,0,2,1:T(8,128)} %bitcast.330), calls=%async_computation.1 | async-start | bytes 4194304 | tf_op jit(solution)/shard_map/all_to_all | solution.py:103
  122.2 154.4 %all-gather.6.cloned.1.call-start = ((), (), s32[]{:S(2)}) async-start(), calls=%async_computation.5 | async-start | bytes 4325376 | tf_op jit(solution)/shard_map/all_gather | solution.py:66
  125.5 4.9 copy-start.26
  173.2 89.1 %copy-start.28 = (f32[32]{0:T(128)S(1)}, f32[32]{0:T(128)}, u32[]{:S(2)}) copy-start(f32[32]{0:T(128)} %param.18) | copy-start | bytes 388
  285.0 2.4 copy-start.12
  285.0 2.4 copy-start.23
  287.5 3.0 copy-start.2
  299.0 41.3 %all-to-all-start.2 = ((f32[32,32,4,128]{3,0,2,1:T(8,128)}), f32[32,32,4,128]{3,0,2,1:T(8,128)}, u32[]{:S(2)}, u32[]{:S(2)}) async-start(f32[32,32,4,128]{3,0,2,1:T(8,128)} %bitcast.331), calls=%async_computation.2 | async-start | bytes 4194304 | tf_op jit(solution)/shard_map/all_to_all | solution.py:103
  303.8 144.6 %all-gather.8.cloned.1.call-start = ((), (), s32[]{:S(2)}) async-start(), calls=%async_computation.6 | async-start | bytes 4325376 | tf_op jit(solution)/shard_map/all_gather | solution.py:66
  340.3 3.0 copy-start.24
  456.9 2.4 copy-start.6
  456.9 2.4 copy-start.7
  456.9 2.5 copy-start.8
  456.9 2.5 copy-start.21
  471.7 112.4 %all-to-all-start.3 = ((f32[32,32,4,128]{3,0,2,1:T(8,128)}), f32[32,32,4,128]{3,0,2,1:T(8,128)}, u32[]{:S(2)}, u32[]{:S(2)}) async-start(f32[32,32,4,128]{3,0,2,1:T(8,128)} %bitcast.329), calls=%async_computation.3 | async-start | bytes 4194304 | tf_op jit(solution)/shard_map/all_to_all | solution.py:103
  (12 other events, 15.2 us)
Sparse Core Ops, SparseCore 0:
  11.2 83.0 all-gather.3
  175.4 78.8 all-gather.5
  345.4 77.5 all-gather.7
where the time goes:
time: 606 us; the launch traced here: 597 us
  blocking collectives  269 us (44%)
  waiting for transfers between devices  122 us (20%)
  matrix products  85.9 us (14%)
  local copies, waits for them, and re-layouts  50.6 us (8%)
  other arithmetic  25.8 us (4%)
  starting transfers between devices  25.4 us (4%)
  between operations  18.5 us (3%)
    psum x3, blocking collectives, per_device(): losses = lax.psum(partial_value, 'net')  229 us
    all_to_all x3, waiting for transfers between devices, per_device(): lax.all_to_all(term_pack.reshape(scen_rows, net_size, slot_cap, block_row...  62.9 us
    all_gather x3, waiting for transfers between devices, per_device(): gathered = lax.all_gather(dual_panel, 'net', axis=1, tiled=True)  58.6 us
    dot_general x12, matrix products, per_device(): jnp.einsum('sjn,jmn->sjm', local_rows, local_blocks[:, touched], preferre...  41.3 us
    psum x3, blocking collectives, per_device(): mean_risk = lax.psum(jnp.sum(risk_now), 'scen') / scen_total  40 us
    all_to_all x3, starting transfers between devices, per_device(): lax.all_to_all(term_pack.reshape(scen_rows, net_size, slot_cap, block_row...  15 us
    reshape x3, local copies, waits for them, and re-layouts, per_device(): gathered.reshape(scen_rows, -1, block_rows)  14.6 us
    dot_general x3, matrix products, per_device(): jnp.einsum('sjm,jkmn->sjkn', flow_grid, local_blocks, preferred_element_t...  14.5 us
  transfers between devices with their start and end apart: 7, of which 3 were waited for; matrix products, arithmetic and copies ran while one was open for 17% of the time, Pallas kernels for 0%

commit v1 on v0

--- a/solution.py
+++ b/solution.py
@@ -100,12 +100,20 @@
         term_pack = jnp.where(
             slot_filled[None, :, None], jnp.take(own_terms, slot_source, axis=1), 0.0
         )
-        arrived = lax.all_to_all(
-            term_pack.reshape(scen_rows, net_size, slot_cap, block_rows),
-            "net",
-            split_axis=1,
-            concat_axis=1,
-            tiled=True,
+        arrived = jnp.concatenate(
+            lax.all_to_all(
+                jnp.stack(
+                    jnp.split(
+                        term_pack.reshape(scen_rows, net_size, slot_cap, block_rows),
+                        lax.axis_size("net"),
+                        axis=1,
+                    )
+                ),
+                "net",
+                0,
+                0,
+            ),
+            axis=1,
         )
         head_terms = arrived.reshape(scen_rows, slot_count, block_rows)
         summed = jnp.einsum("sqn,qb->sbn", head_terms, asked_wide, precision=select_prec)

time: 606 us -> 663 us (1.094)
  local copies, waits for them, and re-layouts: 50.6 us -> 111 us
    unnamed x64 -> x157, local copies, waits for them, and re-layouts: 5.36 us -> 63.9 us
    all_to_all x3 -> x0, local copies, waits for them, and re-layouts: 8.87 us -> none  [per_device(): lax.all_to_all(term_pack.reshape(scen_rows, net_size, slot_cap, block_row...]
    reshape x0 -> x3, local copies, waits for them, and re-layouts: none -> 8.87 us  [per_device(): jnp.concatenate(lax.all_to_all(jnp.stack(jnp.split(term_pack.reshape(scen...]
  transfers between devices with their start and end apart: 7 -> 7, of which waited for: 3 -> 3; matrix products, arithmetic and copies ran while one was open for 17% -> 18% of each run, Pallas kernels for 0% -> 0%
where the time goes in v1:
time: 663 us; the launch traced here: 655 us
  blocking collectives  269 us (41%)
  waiting for transfers between devices  122 us (18%)
  local copies, waits for them, and re-layouts  111 us (17%)
  matrix products  86 us (13%)
  starting transfers between devices  25.4 us (4%)
  other arithmetic  22.9 us (3%)
  between operations  18.6 us (3%)
    psum x3, blocking collectives, per_device(): losses = lax.psum(partial_value, 'net')  229 us
    unnamed x157, local copies, waits for them, and re-layouts  63.9 us
    all_to_all x3, waiting for transfers between devices, per_device(): lax.all_to_all(jnp.stack(jnp.split(term_pack.reshape(scen_rows, net_size,...  63 us
    all_gather x3, waiting for transfers between devices, per_device(): gathered = lax.all_gather(dual_panel, 'net', axis=1, tiled=True)  58.6 us
    dot_general x12, matrix products, per_device(): jnp.einsum('sjn,jmn->sjm', local_rows, local_blocks[:, touched], preferre...  41.3 us
    psum x3, blocking collectives, per_device(): mean_risk = lax.psum(jnp.sum(risk_now), 'scen') / scen_total  40 us
    all_to_all x3, starting transfers between devices, per_device(): lax.all_to_all(jnp.stack(jnp.split(term_pack.reshape(scen_rows, net_size,...  15 us
    reshape x3, local copies, waits for them, and re-layouts, per_device(): gathered.reshape(scen_rows, -1, block_rows)  14.6 us
  transfers between devices with their start and end apart: 7, of which 3 were waited for; matrix products, arithmetic and copies ran while one was open for 18% of the time, Pallas kernels for 0%

profile of v1, /device:TPU:0, one launch (start us, length us, event | category | flops | bytes accessed | tf_op | source)
XLA Modules:
  0.0 655.0 jit_solution(1158202875819392403)
XLA Ops:
  10.9 9.6 %all-to-all-start = ((s32[32,1,4]{2,1,0:T(1,128)}), s32[32,1,4]{2,1,0:T(1,128)S(1)}, u32[]{:S(2)}, u32[]{:S(2)}) async-start(s32[32,1,4]{2,1,0:T(1,128)} %bitcast.20), calls=%async_computation | async-start | bytes 32768 | tf_op jit(solution)/shard_map/all_to_all | solution.py:52
  27.9 3.8 fusion.16
  31.7 3.9 fusion.22
  35.6 58.6 %all-gather.4.cloned.1.call-done = bf16[32,65536]{1,0:T(8,128)(2,1)} async-done(((bf16[32,2048]{1,0:T(8,128)(2,1)}), bf16[32,65536]{1,0:T(8,128)(2,1)}) %all-gather.4.cloned.1.call-update) | async-done | bytes 4194320 | tf_op jit(solution)/shard_map/all_gather | solution.py:66
  94.2 4.9 copy_bitcast_fusion.2
  136.0 5.4 all-to-all-start.1
  144.8 4.8 convolution_bitcast_fusion.2
  152.7 36.8 %all-to-all-done.1 = f32[32,32,1,4,128]{4,1,3,2,0:T(8,128)} async-done(((f32[32,32,1,4,128]{4,1,3,2,0:T(8,128)}), f32[32,32,1,4,128]{4,1,3,2,0:T(8,128)}, u32[]{:S(2)}, u32[]{:S(2)}) %all-to-all-start.1) | async-done | bytes 2097184 | tf_op jit(solution)/shard_map/all_to_all | solution.py:104
  195.1 13.0 %psum.43 = f32[]{:T(128)} all-reduce(f32[]{:T(128)} %reduce_sum.64), channel_id=1, replica_groups=mesh['net'=32,'scen'=8] {'scen'}, use_global_device_ids=true, to_apply=%region_3.5 | all-reduce | flops 1 | bytes 8 | tf_op jit(solution)/shard_map/psum | solution.py:83
  209.4 72.1 %psum.42 = f32[32]{0:T(128)S(1)} all-reduce(f32[32]{0:T(128)S(1)} %broadcast_multiply_fusion.2), channel_id=1, replica_groups=mesh['net'=32,'scen'=8] {'net'}, use_global_device_ids=true, to_apply=%region_1.3 | all-reduce | flops 32 | bytes 256 | tf_op jit(solution)/shard_map/psum | solution.py:93
  288.1 3.9 fusion.14
  295.8 4.9 copy_bitcast_fusion.1
  337.4 4.8 all-to-all-start.2
  343.9 4.8 convolution_bitcast_fusion.1
  352.6 26.2 %all-to-all-done.2 = f32[32,32,1,4,128]{4,1,3,2,0:T(8,128)} async-done(((f32[32,32,1,4,128]{4,1,3,2,0:T(8,128)}), f32[32,32,1,4,128]{4,1,3,2,0:T(8,128)}, u32[]{:S(2)}, u32[]{:S(2)}) %all-to-all-start.2) | async-done | bytes 2097184 | tf_op jit(solution)/shard_map/all_to_all | solution.py:104
  383.8 13.1 %psum.45 = f32[]{:T(128)} all-reduce(f32[]{:T(128)} %get-tuple-element.16), channel_id=1, replica_groups=mesh['net'=32,'scen'=8] {'scen'}, use_global_device_ids=true, to_apply=%region_11.14 | all-reduce | flops 1 | bytes 8 | tf_op jit(solution)/shard_map/psum | solution.py:83
  397.5 74.1 %psum.44 = f32[32]{0:T(128)S(1)} all-reduce(f32[32]{0:T(128)S(1)} %broadcast_multiply_fusion.1), channel_id=1, replica_groups=mesh['net'=32,'scen'=8] {'net'}, use_global_device_ids=true, to_apply=%region_9.12 | all-reduce | flops 32 | bytes 256 | tf_op jit(solution)/shard_map/psum | solution.py:93
  475.4 3.8 fusion.6
  479.2 3.9 fusion.12
  486.9 4.9 copy_bitcast_fusion
  529.4 4.8 all-to-all-start.3
  534.1 13.9 %psum.47 = f32[]{:T(128)} all-reduce(f32[]{:T(128)} %get-tuple-element.11), channel_id=1, replica_groups=mesh['net'=32,'scen'=8] {'scen'}, use_global_device_ids=true, to_apply=%region_15.18 | all-reduce | flops 1 | bytes 8 | tf_op jit(solution)/shard_map/psum | solution.py:83
  550.1 83.1 %psum.46 = f32[32]{0:T(128)S(1)} all-reduce(f32[32]{0:T(128)S(1)} %broadcast_multiply_fusion), channel_id=1, replica_groups=mesh['net'=32,'scen'=8] {'net'}, use_global_device_ids=true, to_apply=%region_13.16 | all-reduce | flops 32 | bytes 256 | tf_op jit(solution)/shard_map/psum | solution.py:93
  633.8 4.8 convolution_bitcast_fusion
  (247 shorter events, 172.5 us)
Async XLA Ops:
  7.2 95.6 %copy-start = (bf16[64,128,128]{2,1,0:T(8,128)(2,1)S(1)}, bf16[64,128,128]{2,1,0:T(8,128)(2,1)}, u32[]{:S(2)}) copy-start(bf16[64,128,128]{2,1,0:T(8,128)(2,1)} %param.23) | copy-start | bytes 6291460
  7.2 87.1 %all-gather.4.cloned.1.call-start = ((), (), s32[]{:S(2)}) async-start(), calls=%async_computation.4 | async-start | bytes 4325376 | tf_op jit(solution)/shard_map/all_gather | solution.py:66
  10.9 125.1 %all-to-all-start = ((s32[32,1,4]{2,1,0:T(1,128)}), s32[32,1,4]{2,1,0:T(1,128)S(1)}, u32[]{:S(2)}, u32[]{:S(2)}) async-start(s32[32,1,4]{2,1,0:T(1,128)} %bitcast.20), calls=%async_computation | async-start | bytes 32768 | tf_op jit(solution)/shard_map/all_to_all | solution.py:52
  102.7 2.4 copy-start.11
  102.7 2.5 copy-start.22
  105.2 3.0 copy-start.3
  105.2 3.0 copy-start.25
  105.2 3.0 copy-start.27
  108.8 34.5 %copy-start.1 = (f32[32,8192]{1,0:T(8,128)}, f32[32,8192]{1,0:T(8,128)S(1)}, u32[]{:S(2)}) copy-start(f32[32,8192]{1,0:T(8,128)S(1)} %get-tuple-element.21) | copy-start | bytes 3145732
  136.0 53.5 %all-to-all-start.1 = ((f32[32,32,1,4,128]{4,1,3,2,0:T(8,128)}), f32[32,32,1,4,128]{4,1,3,2,0:T(8,128)}, u32[]{:S(2)}, u32[]{:S(2)}) async-start(f32[32,32,1,4,128]{4,1,3,2,0:T(8,128)} %constant_dynamic-update-slice_fusion), calls=%async_computation.1 | async-start | bytes 4194304 | tf_op jit(solution)/shard_map/all_to_all | solution.py:104
  141.4 154.3 %all-gather.6.cloned.1.call-start = ((), (), s32[]{:S(2)}) async-start(), calls=%async_computation.5 | async-start | bytes 4325376 | tf_op jit(solution)/shard_map/all_gather | solution.py:66
  144.8 4.9 copy-start.26
  192.5 89.1 %copy-start.28 = (f32[32]{0:T(128)S(1)}, f32[32]{0:T(128)}, u32[]{:S(2)}) copy-start(f32[32]{0:T(128)} %param.18) | copy-start | bytes 388
  304.2 2.4 copy-start.12
  304.2 2.4 copy-start.23
  306.7 3.0 copy-start.2
  337.4 41.3 %all-to-all-start.2 = ((f32[32,32,1,4,128]{4,1,3,2,0:T(8,128)}), f32[32,32,1,4,128]{4,1,3,2,0:T(8,128)}, u32[]{:S(2)}, u32[]{:S(2)}) async-start(f32[32,32,1,4,128]{4,1,3,2,0:T(8,128)} %constant_dynamic-update-slice_fusion.32), calls=%async_computation.2 | async-start | bytes 4194304 | tf_op jit(solution)/shard_map/all_to_all | solution.py:104
  342.2 144.7 %all-gather.8.cloned.1.call-start = ((), (), s32[]{:S(2)}) async-start(), calls=%async_computation.6 | async-start | bytes 4325376 | tf_op jit(solution)/shard_map/all_gather | solution.py:66
  378.7 3.0 copy-start.24
  495.3 2.4 copy-start.6
  495.3 2.4 copy-start.7
  495.3 2.5 copy-start.8
  495.3 2.5 copy-start.21
  529.4 112.4 %all-to-all-start.3 = ((f32[32,32,1,4,128]{4,1,3,2,0:T(8,128)}), f32[32,32,1,4,128]{4,1,3,2,0:T(8,128)}, u32[]{:S(2)}, u32[]{:S(2)}) async-start(f32[32,32,1,4,128]{4,1,3,2,0:T(8,128)} %constant_dynamic-update-slice_fusion.64), calls=%async_computation.3 | async-start | bytes 4194304 | tf_op jit(solution)/shard_map/all_to_all | solution.py:104
  (12 other events, 15.2 us)
Sparse Core Ops, SparseCore 0:
  11.2 83.0 all-gather.3
  194.6 78.8 all-gather.5
  383.9 77.5 all-gather.7
